TPU v7x, 128 devices: a whole 4x4x4 slice. The times are simulated.
128 devices in a mesh: inner: 8 (over z, core), outer: 16 (over x, y).
Axes of the slice: x: 4, y: 4, z: 4, core: 2. Of those that a mesh axis runs over, the one named last changes fastest.
Arguments:
- inputs: bfloat16 [131072, 4096], P(('inner', 'outer')), may hold values from -6 to 6
- cotangent: bfloat16 [131072, 4096], P(('inner', 'outer')), may hold values from -0.176776695 to 0.176776695
- weights: bfloat16 [2, 64, 128, 128], replicated, may hold values from -0.375 to 0.375
- block_rows: int32 [2, 64], replicated, may hold values from 0 to 31, as said below
- block_cols: int32 [2, 64], replicated, may hold values from 0 to 31, as said below
- momentum: float32 [2, 8192, 128], P(None, ('inner', 'outer')), may hold values from -6 to 6
Outputs:
- new_weights: bfloat16 [2, 8192, 128], P(None, ('inner', 'outer'))
- new_momentum: float32 [2, 8192, 128], P(None, ('inner', 'outer'))
Inputs may be any that keep to these rules, and one draw needn't show every extreme that they name: For each p the 64 pairs (block_rows[p, n], block_cols[p, n]) are distinct. `block_cols`: see block_rows.
All inputs are finite; a program needn't handle non-finite values.
Results may differ from a plain program's by a relative error of at most 0.01.
Values may be sent and summed in bfloat16 or wider, within the bound.
A program may use at most 320 MiB of HBM per device.

v0:
```python
import jax
import jax.numpy as jnp
from jax import lax
from jax.sharding import PartitionSpec as P

dot_epsilon = 1e-06
momentum_decay = 0.9
step_rate = 0.05
root_half = 0.7071067811865476
inv_root_tau = 0.3989422804014327


def from_partner(array, axis, distance):
    return lax.ppermute(array, axis, [(i, i ^ 1 << distance) for i in range(lax.axis_size(axis))])


def one_hot_table(indices, total_count, dtype):
    return (indices[:, None] == jnp.arange(total_count, dtype=jnp.int32)[None, :]).astype(dtype)


def pick_blocks(blocked, table):
    picked = jnp.einsum("tcb,nc->tnb", blocked, table, preferred_element_type=jnp.float32)
    return picked.astype(jnp.bfloat16)


def place_blocks(block_terms, table):
    return jnp.einsum(
        "tnj,nc->tcj",
        block_terms,
        table,
        precision=lax.Precision.HIGHEST,
        preferred_element_type=jnp.float32,
    )


def pair_moments(lower_part, upper_part):
    return jnp.stack(
        [
            jnp.sum(lower_part * upper_part, axis=(1, 2)),
            jnp.sum(lower_part * lower_part, axis=(1, 2)),
            jnp.sum(upper_part * upper_part, axis=(1, 2)),
        ]
    )


def adasum_mix(lower_part, upper_part, moments):
    cross = moments[0][:, None, None]
    lower_coef = 1.0 - cross / (2.0 * (moments[1][:, None, None] + dot_epsilon))
    upper_coef = 1.0 - cross / (2.0 * (moments[2][:, None, None] + dot_epsilon))
    return lower_coef * lower_part + upper_coef * upper_part


def local(inputs, cotangent, weights, block_rows, block_cols, momentum):
    rows_here = inputs.shape[0]
    block_size = weights.shape[2]
    column_blocks = inputs.shape[1] // block_size
    rows_first = one_hot_table(block_rows[0], column_blocks, jnp.bfloat16)
    rows_second = one_hot_table(block_rows[1], column_blocks, jnp.bfloat16)
    cols_first = one_hot_table(block_cols[0], column_blocks, jnp.bfloat16)
    cols_second = one_hot_table(block_cols[1], column_blocks, jnp.bfloat16)
    token_blocks = pick_blocks(inputs.reshape(rows_here, column_blocks, block_size), rows_first)
    first_terms = jnp.einsum(
        "tnk,nkj->tnj", token_blocks, weights[0], preferred_element_type=jnp.float32
    )
    hidden = place_blocks(first_terms, cols_first.astype(jnp.float32))
    cumulative = 0.5 * (1.0 + jax.scipy.special.erf(hidden * root_half))
    activated = (hidden * cumulative).astype(jnp.bfloat16)
    gelu_slope = cumulative + hidden * jnp.exp(-0.5 * hidden * hidden) * inv_root_tau
    cot_blocks = pick_blocks(cotangent.reshape(rows_here, column_blocks, block_size), cols_second)
    back_terms = jnp.einsum(
        "tnj,nkj->tnk", cot_blocks, weights[1], preferred_element_type=jnp.float32
    )
    grad_act = place_blocks(back_terms, rows_second.astype(jnp.float32))
    grad_hidden = (grad_act * gelu_slope).astype(jnp.bfloat16)
    second_grad = jnp.einsum(
        "tnk,tnj->nkj",
        pick_blocks(activated, rows_second),
        cot_blocks,
        preferred_element_type=jnp.float32,
    )
    first_grad = jnp.einsum(
        "tnk,tnj->nkj",
        token_blocks,
        pick_blocks(grad_hidden, cols_first),
        preferred_element_type=jnp.float32,
    )
    summed = lax.psum_scatter(
        jnp.stack([first_grad, second_grad]).astype(jnp.bfloat16),
        "inner",
        scatter_dimension=1,
        tiled=True,
    ).astype(jnp.float32)
    own_count = summed.shape[1]
    flattened = summed.reshape(2, own_count * block_size, block_size)
    outer_count = lax.axis_size("outer")
    levels = outer_count.bit_length() - 1
    position = lax.axis_index("outer")
    piece_rows = own_count * block_size // outer_count
    current = flattened
    for level_bit in range(levels):
        partner = from_partner(current.astype(jnp.bfloat16), "outer", level_bit).astype(
            current.dtype
        )
        upper_side = position >> level_bit & 1 == 1
        lower_part = jnp.where(upper_side, partner, current)
        upper_part = jnp.where(upper_side, current, partner)
        current = adasum_mix(lower_part, upper_part, pair_moments(lower_part, upper_part))
    combined = lax.dynamic_slice_in_dim(current, position * piece_rows, piece_rows, 1)
    new_momentum = momentum_decay * momentum + combined
    inner_index = lax.axis_index("inner")
    stacked_weights = weights.reshape(2, -1, block_size)
    owned_weights = lax.dynamic_slice_in_dim(
        stacked_weights, (inner_index * outer_count + position) * piece_rows, piece_rows, 1
    )
    new_weights = (owned_weights.astype(jnp.float32) - step_rate * new_momentum).astype(
        jnp.bfloat16
    )
    return (new_weights, new_momentum)


def solution(mesh):
    return jax.shard_map(
        local,
        mesh=mesh,
        in_specs=(
            P(("inner", "outer"), None),
            P(("inner", "outer"), None),
            P(),
            P(),
            P(),
            P(None, ("inner", "outer"), None),
        ),
        out_specs=(P(None, ("inner", "outer"), None), P(None, ("inner", "outer"), None)),
        check_vma=False,
    )
```

profile of v0, /device:TPU:96, one launch (start us, length us, event | category | flops | bytes accessed | tf_op | source)
XLA Modules:
  0.0 428.3 jit_solution(5233833778793266857)
XLA Ops:
  7.2 0.0 copy-start.1
  7.2 0.0 reduce-scatter.5.cloned.1.call-start
  7.2 0.0 copy-start.2
  7.2 9.5 %copy.20 = bf16[128,8,32,128]{3,2,1,0:T(8,128)(2,1)} copy(bf16[128,8,32,128]{3,1,2,0:T(8,128)(2,1)} %bitcast.117) | data formatting | bytes 16777216
  16.7 0.0 copy-done.1
  16.8 9.4 %copy.19 = bf16[128,8,32,128]{3,2,1,0:T(8,128)(2,1)} copy(bf16[128,8,32,128]{3,1,2,0:T(8,128)(2,1)} %bitcast.118) | data formatting | bytes 16777216
  26.2 0.0 copy-done.2
  26.2 13.6 %convert_bitcast_fusion.1 = bf16[1024,64,128]{2,1,0:T(8,128)(2,1)} fusion(bf16[1024,32,128]{2,1,0:T(8,128)(2,1)} %bitcast.113, s32[64]{0:T(128)S(1)} %get-tuple-element.21), kind=kOutput, calls=%fused_computation.25 | convolution fusion | flops 545261568 | bytes 25166080 | tf_op jit(solution)/shard_map/tcb,nc->tnb/dot_general | solution.py:22
  39.8 23.3 %copy.10 = bf16[1024,64,128]{0,2,1:T(8,128)(2,1)} copy(bf16[1024,64,128]{2,1,0:T(8,128)(2,1)} %convert_bitcast_fusion.1) | data formatting | bytes 33554432 | tf_op jit(solution)/shard_map/convert_element_type | solution.py:23
  63.1 18.4 %fusion.31 = f32[64,1024,128]{2,1,0:T(8,128)} fusion(bf16[1024,64,128]{0,2,1:T(8,128)(2,1)} %copy.10, bf16[2,64,128,128]{3,2,1,0:T(8,128)(2,1)} %param.8), kind=kOutput, calls=%fused_computation.33 | convolution fusion | flops 2147483648 | bytes 52428800 | tf_op jit(solution)/shard_map/tnk,nkj->tnj/dot_general | solution.py:62
  81.5 39.9 %fusion = f32[32,1024,128]{2,0,1:T(8,128)} fusion(f32[64,1024,128]{2,1,0:T(8,128)} %fusion.31, s32[64]{0:T(128)S(1)} %get-tuple-element.22), kind=kOutput, calls=%fused_computation | convolution fusion | flops 3221227520 | bytes 50331904 | tf_op jit(solution)/shard_map/tnj,nc->tcj/dot_general | solution.py:27
  121.5 15.0 %fusion.29 = bf16[64,1024,128]{2,0,1:T(8,128)(2,1)} fusion(f32[32,1024,128]{2,0,1:T(8,128)} %fusion, s32[64]{0:T(128)S(1)} %get-tuple-element.20), kind=kOutput, calls=%fused_computation.30 | convolution fusion | flops 557844480 | bytes 33554688 | tf_op jit(solution)/shard_map/tcb,nc->tnb/dot_general | solution.py:22
  136.4 23.1 %copy.16 = bf16[64,1024,128]{1,2,0:T(8,128)(2,1)} copy(bf16[64,1024,128]{2,0,1:T(8,128)(2,1)} %fusion.29) | data formatting | bytes 33554432 | tf_op jit(solution)/shard_map/tcb,nc->tnb/dot_general | solution.py:22
  159.6 13.7 %convert_bitcast_fusion = bf16[1024,64,128]{2,1,0:T(8,128)(2,1)} fusion(bf16[1024,32,128]{2,1,0:T(8,128)(2,1)} %bitcast.112, s32[64]{0:T(128)S(1)} %get-tuple-element.23), kind=kOutput, calls=%fused_computation.24 | convolution fusion | flops 545261568 | bytes 25166080 | tf_op jit(solution)/shard_map/tcb,nc->tnb/dot_general | solution.py:22
  173.3 25.8 %fusion.24 = f32[1024,64,128]{2,0,1:T(8,128)} fusion(bf16[1024,64,128]{2,1,0:T(8,128)(2,1)} %convert_bitcast_fusion, bf16[2,64,128,128]{3,2,1,0:T(8,128)(2,1)} %param.8), kind=kOutput, calls=%fused_computation.29 | convolution fusion | flops 2147483648 | bytes 52428800 | tf_op jit(solution)/shard_map/tnj,nkj->tnk/dot_general | solution.py:70
  199.1 25.9 %convert_bitcast_fusion.2 = bf16[1,64,128,128]{3,2,1,0:T(8,128)(2,1)S(1)} fusion(bf16[1024,64,128]{2,1,0:T(8,128)(2,1)} %convert_bitcast_fusion, bf16[64,1024,128]{1,2,0:T(8,128)(2,1)} %copy.16), kind=kOutput, calls=%fused_computation.36 | convolution fusion | flops 2148532224 | bytes 35651584 | tf_op jit(solution)/shard_map/tnk,tnj->nkj/dot_general | solution.py:75
  225.0 49.8 %fusion.10 = bf16[1024,32,128]{2,1,0:T(8,128)(2,1)} fusion(f32[32,1024,128]{2,0,1:T(8,128)} %fusion, f32[1024,64,128]{2,0,1:T(8,128)} %fusion.24, s32[64]{0:T(128)S(1)} %get-tuple-element.20), kind=kOutput, calls=%fused_computation.12 | convolution fusion | flops 3263170560 | bytes 58720512 | tf_op jit(solution)/shard_map/tnj,nc->tcj/dot_general | solution.py:27
  274.8 13.6 %fusion.52 = bf16[64,1024,128]{2,0,1:T(8,128)(2,1)} fusion(bf16[1024,32,128]{2,1,0:T(8,128)(2,1)} %fusion.10, s32[64]{0:T(128)S(1)} %get-tuple-element.22), kind=kOutput, calls=%fused_computation.77 | convolution fusion | flops 536872960 | bytes 25166080 | tf_op jit(solution)/shard_map/tcb,nc->tnb/dot_general | solution.py:22
  288.5 25.8 %convert_bitcast_fusion.3 = bf16[1,64,128,128]{3,2,1,0:T(8,128)(2,1)S(1)} fusion(bf16[1024,64,128]{0,2,1:T(8,128)(2,1)} %copy.10, bf16[64,1024,128]{2,0,1:T(8,128)(2,1)} %fusion.52), kind=kOutput, calls=%fused_computation.37 | convolution fusion | flops 2148532224 | bytes 35651584 | tf_op jit(solution)/shard_map/tnk,tnj->nkj/dot_general | solution.py:81
  314.3 0.4 pad_maximum_fusion
  314.7 0.0 copy-start
  314.7 0.6 copy.17
  315.2 4.8 %copy.47 = bf16[8,8,256,128]{3,1,2,0:T(8,128)(2,1)} copy(bf16[8,8,256,128]{3,2,1,0:T(8,128)(2,1)S(1)} %bitcast.115) | data formatting | bytes 8388608
  320.0 0.0 reduce-scatter.5.cloned.1.call-update
  320.0 35.9 %reduce-scatter.5.cloned.1.call-done = bf16[8,32768]{1,0:T(8,128)(2,1)} async-done(((bf16[64,32768]{1,0:T(8,128)(2,1)}), bf16[8,32768]{1,0:T(8,128)(2,1)}) %reduce-scatter.5.cloned.1.call-update) | async-done | bytes 524304
  355.9 1.1 copy.18
  357.1 1.5 collective-permute-start
  358.6 12.5 %collective-permute-done = bf16[2,1024,128]{2,1,0:T(8,128)(2,1)S(1)} collective-permute-done((bf16[2,1024,128]{2,1,0:T(8,128)(2,1)S(1)}, bf16[2,1024,128]{2,1,0:T(8,128)(2,1)S(1)}, u32[]{:S(2)}, u32[]{:S(2)}) %collective-permute-start) | collective-permute-done | bytes 524320 | tf_op jit(solution)/shard_map/ppermute | solution.py:14
  371.1 0.7 multiply_reduce_fusion.10
  371.8 0.3 fusion.70
  372.2 3.1 collective-permute-start.1
  375.2 13.0 %collective-permute-done.1 = bf16[2,1024,128]{2,1,0:T(8,128)(2,1)S(1)} collective-permute-done((bf16[2,1024,128]{2,1,0:T(8,128)(2,1)S(1)}, bf16[2,1024,128]{2,1,0:T(8,128)(2,1)S(1)}, u32[]{:S(2)}, u32[]{:S(2)}) %collective-permute-start.1) | collective-permute-done | bytes 524320 | tf_op jit(solution)/shard_map/ppermute | solution.py:14
  388.2 0.9 multiply_reduce_fusion.7
  389.2 0.5 fusion.73
  389.7 1.5 collective-permute-start.2
  391.2 12.2 %collective-permute-done.2 = bf16[2,1024,128]{2,1,0:T(8,128)(2,1)S(1)} collective-permute-done((bf16[2,1024,128]{2,1,0:T(8,128)(2,1)S(1)}, bf16[2,1024,128]{2,1,0:T(8,128)(2,1)S(1)}, u32[]{:S(2)}, u32[]{:S(2)}) %collective-permute-start.2) | collective-permute-done | bytes 524320 | tf_op jit(solution)/shard_map/ppermute | solution.py:14
  403.4 0.6 multiply_reduce_fusion.4
  404.0 0.3 fusion.69
  404.3 3.0 collective-permute-start.3
  407.3 11.4 %collective-permute-done.3 = bf16[2,1024,128]{2,1,0:T(8,128)(2,1)S(1)} collective-permute-done((bf16[2,1024,128]{2,1,0:T(8,128)(2,1)S(1)}, bf16[2,1024,128]{2,1,0:T(8,128)(2,1)S(1)}, u32[]{:S(2)}, u32[]{:S(2)}) %collective-permute-start.3) | collective-permute-done | bytes 524320 | tf_op jit(solution)/shard_map/ppermute | solution.py:14
  418.7 0.8 multiply_reduce_fusion.1
  419.5 0.0 copy-done
  419.5 1.5 subtract_convert_fusion
  (6 shorter events, 0.1 us)
Async XLA Ops:
  7.2 9.6 %copy-start.1 = (s32[2,64]{1,0:T(2,128)S(1)}, s32[2,64]{1,0:T(2,128)}, u32[]{:S(2)}) copy-start(s32[2,64]{1,0:T(2,128)} %param.10) | copy-start | bytes 1540
  7.2 348.8 %reduce-scatter.5.cloned.1.call-start = ((), (), s32[]{:S(2)}) async-start(), calls=%async_computation.1 | async-start | bytes 4718592
  7.2 19.0 %copy-start.2 = (s32[2,64]{1,0:T(2,128)S(1)}, s32[2,64]{1,0:T(2,128)}, u32[]{:S(2)}) copy-start(s32[2,64]{1,0:T(2,128)} %param.9) | copy-start | bytes 1540
  314.7 104.9 %copy-start = (f32[2,64,128]{2,1,0:T(8,128)S(1)}, f32[2,64,128]{2,1,0:T(8,128)}, u32[]{:S(2)}) copy-start(f32[2,64,128]{2,1,0:T(8,128)} %param.11) | copy-start | bytes 196612
  357.1 14.1 %collective-permute-start = (bf16[2,1024,128]{2,1,0:T(8,128)(2,1)S(1)}, bf16[2,1024,128]{2,1,0:T(8,128)(2,1)S(1)}, u32[]{:S(2)}, u32[]{:S(2)}) collective-permute-start(bf16[2,1024,128]{2,1,0:T(8,128)(2,1)S(1)} %bitcast.116), channel_id=1, source_target_pairs={{0,1},{1,0},{2,3},{3,2},{4,5},{5,4},{6,7},{7,6},{8,9},{9,8},{10,11... | collective-permute-start | bytes 1572872 | tf_op jit(solution)/shard_map/ppermute | solution.py:14
  372.2 16.1 %collective-permute-start.1 = (bf16[2,1024,128]{2,1,0:T(8,128)(2,1)S(1)}, bf16[2,1024,128]{2,1,0:T(8,128)(2,1)S(1)}, u32[]{:S(2)}, u32[]{:S(2)}) collective-permute-start(bf16[2,1024,128]{2,1,0:T(8,128)(2,1)S(1)} %fusion.70), channel_id=1, source_target_pairs={{0,2},{1,3},{2,0},{3,1},{4,6},{5,7},{6,4},{7,5},{8,10},{9,11},{10,... | collective-permute-start | bytes 1572872 | tf_op jit(solution)/shard_map/ppermute | solution.py:14
  389.7 13.7 %collective-permute-start.2 = (bf16[2,1024,128]{2,1,0:T(8,128)(2,1)S(1)}, bf16[2,1024,128]{2,1,0:T(8,128)(2,1)S(1)}, u32[]{:S(2)}, u32[]{:S(2)}) collective-permute-start(bf16[2,1024,128]{2,1,0:T(8,128)(2,1)S(1)} %get-tuple-element.18), channel_id=1, source_target_pairs={{0,4},{1,5},{2,6},{3,7},{4,0},{5,1},{6,2},{7,3},{8,12},{9,13},{10,... | collective-permute-start | bytes 1572872 | tf_op jit(solution)/shard_map/ppermute | solution.py:14
  404.3 14.3 %collective-permute-start.3 = (bf16[2,1024,128]{2,1,0:T(8,128)(2,1)S(1)}, bf16[2,1024,128]{2,1,0:T(8,128)(2,1)S(1)}, u32[]{:S(2)}, u32[]{:S(2)}) collective-permute-start(bf16[2,1024,128]{2,1,0:T(8,128)(2,1)S(1)} %fusion.69), channel_id=1, source_target_pairs={{0,8},{1,9},{2,10},{3,11},{4,12},{5,13},{6,14},{7,15},{8,0},{9,1},... | collective-permute-start | bytes 1572872 | tf_op jit(solution)/shard_map/ppermute | solution.py:14
Sparse Core Ops, SparseCore 0:
  320.2 35.7 reduce-scatter.4
where the time goes:
time: 436 us; the launch traced here: 428 us
  matrix products  242 us (56%)
  waiting for transfers between devices  85 us (19%)
  local copies, waits for them, and re-layouts  71.9 us (16%)
  between operations  14.6 us (3%)
  starting transfers between devices  9.13 us (2%)
  other arithmetic  6.13 us (1%)
    dot_general x2, matrix products, place_blocks(): jnp.einsum('tnj,nc->tcj', block_terms, table, precision=lax.Precision.HIG...  89.7 us
    dot_general x4, matrix products, pick_blocks(): jnp.einsum('tcb,nc->tnb', blocked, table, preferred_element_type=jnp.floa...  56 us
    ppermute x4, waiting for transfers between devices, from_partner(): lax.ppermute(array, axis, [(i, i ^ 1 << distance) for i in range(lax.axis...  49.1 us
    unnamed x2, waiting for transfers between devices  35.9 us
    dot_general x1, matrix products, local(): jnp.einsum('tnk,tnj->nkj', pick_blocks(activated, rows_second), cot_block...  25.9 us
    dot_general x1, matrix products, local(): jnp.einsum('tnj,nkj->tnk', cot_blocks, weights[1], preferred_element_type...  25.8 us
    dot_general x1, matrix products, local(): jnp.einsum('tnk,tnj->nkj', token_blocks, pick_blocks(grad_hidden, cols_fi...  25.8 us
    unnamed x11, local copies, waits for them, and re-layouts  25.4 us
  transfers between devices with their start and end apart: 5, of which 5 were waited for; matrix products, arithmetic and copies ran while one was open for 0% of the time, Pallas kernels for 0%

commit v1 on v0

v1 whole, which is shorter than its diff:
```python
import functools
import jax
import jax.numpy as jnp
from jax import lax
from jax.sharding import PartitionSpec as P
from jax.experimental import pallas as pl
from jax.experimental.pallas import tpu as pltpu
f32 = jnp.float32
bf = jnp.bfloat16
i32 = jnp.int32
dot_epsilon = 1e-06
momentum_decay = 0.9
step_rate = 0.05
NCB = 32
OWN = 8
ZS = 4
NOUT = 16
PIECE = 64
root_half = 0.7071067811865476
inv_root_tau = 0.3989422804014327

def forward_kernel(sub, rows_ref, cols_ref, x_ref, cot_ref, w_ref, act_ref, gh_ref, head, link, extra_h, extra_a):
    blk=w_ref.shape[2]; nb=w_ref.shape[1]; ncb=x_ref.shape[1]//blk; tile=x_ref.shape[0]
    @pl.when(pl.program_id(0)==0)
    def _():
        extra_h[...]=jnp.zeros_like(extra_h); extra_a[...]=jnp.zeros_like(extra_a)
        def clear(c,_):
            head[0,c]=nb; head[1,c]=nb
            return 0
        lax.fori_loop(0,ncb,clear,0)
        link[0,nb]=nb; link[1,nb]=nb
        def push(n,_):
            c=cols_ref[0,n]; link[0,n]=head[0,c]; head[0,c]=n
            r=rows_ref[1,n]; link[1,n]=head[1,r]; head[1,r]=n
            return 0
        lax.fori_loop(0,nb,push,0)
    def take(p,n):
        safe=jnp.minimum(n,nb-1)
        w=w_ref[p,safe]
        w=jnp.where(n<nb,w,jnp.zeros_like(w))
        feat=rows_ref[0,safe] if p==0 else cols_ref[1,safe]
        return w, pl.ds(pl.multiple_of(feat*blk,blk),blk)
    def pair(p,n,m):
        w1,d1=take(p,n); w2,d2=take(p,m)
        return jnp.concatenate([w1,w2],axis=p), d1, d2
    def product(p,prepared,rows):
        w,d1,d2=prepared
        ref=x_ref if p==0 else cot_ref
        left=jnp.concatenate([ref[rows,d1],ref[rows,d2]],axis=1)
        dims=(((1,),(p,)),((),()))
        return lax.dot_general(left,w,dims,preferred_element_type=f32)
    def column(c,_):
        a0=head[0,c]; b0=link[0,a0]; m0=link[0,b0]
        a1=head[1,c]; b1=link[1,a1]; m1=link[1,b1]
        for p,first,store in ((0,m0,extra_h),(1,m1,extra_a)):
            def more(n,p=p,store=store):
                second=link[p,n]
                got=pair(p,n,second)
                for s in range(0,tile,sub):
                    rows=pl.ds(s,sub)
                    store[rows,:]+=product(p,got,rows)
                return link[p,second]
            lax.while_loop(lambda n: n<nb, more, first)
        got0=pair(0,a0,b0); got1=pair(1,a1,b1)
        for s in range(0,tile,sub):
            rows=pl.ds(s,sub)
            h=product(0,got0,rows)+extra_h[rows,:]
            g=product(1,got1,rows)+extra_a[rows,:]
            cum=0.5*(1.0+lax.erf(h*root_half))
            act_ref[c,rows,:]=(h*cum).astype(bf)
            slope=cum+h*jnp.exp(-0.5*h*h)*inv_root_tau
            gh_ref[c,rows,:]=(g*slope).astype(bf)
        @pl.when(m0<nb)
        def _(): extra_h[...]=jnp.zeros_like(extra_h)
        @pl.when(m1<nb)
        def _(): extra_a[...]=jnp.zeros_like(extra_a)
        return 0
    lax.fori_loop(0,ncb,column,0)

def forward(inputs,cotangent,weights,block_rows,block_cols,tile=512,sub=128):
    T,D=inputs.shape
    nb=weights.shape[1]; ncb=D//weights.shape[2]; blk=weights.shape[2]
    smem=pl.BlockSpec(memory_space=pltpu.SMEM)
    wide=pl.BlockSpec((tile,D),lambda t:(t,0))
    return pl.pallas_call(functools.partial(forward_kernel,sub),
        grid=(T//tile,),
        in_specs=[smem,smem,wide,wide,pl.BlockSpec(weights.shape,lambda t:(0,0,0,0),pipeline_mode=pl.Buffered(1))],
        out_specs=[pl.BlockSpec((ncb,tile,blk),lambda t:(0,t,0))]*2,
        out_shape=[jax.ShapeDtypeStruct((ncb,T,blk),bf)]*2,
        scratch_shapes=[pltpu.SMEM((2,ncb),i32),pltpu.SMEM((2,nb+1),i32),pltpu.VMEM((tile,blk),f32),pltpu.VMEM((tile,blk),f32)],
        compiler_params=pltpu.CompilerParams(vmem_limit_bytes=60*2**20),
        name="forward",
    )(block_rows,block_cols,inputs,cotangent,weights)


def combine_kernel(rows_ref, cols_ref, x_hbm, cot_hbm, act_hbm, gh_hbm, w_hbm, mom_ref, outw_ref, outm_ref,
                   x_v, cot_v, act_v, gh_v, w_v, psend, own, precv, zsend, mid, fin, vsend, pieces, wide, gsend, grecv,
                   load_sem, w_sem, keep_sem, psend_sem, precv_sem, zsend_sem, mid_sem, fin_sem, vsend_sem, vrecv_sem, gsend_sem, grecv_sem):
    MESH = pl.DeviceIdType.MESH
    blk = x_v.shape[2]
    inner = lax.axis_index("inner")
    outer = lax.axis_index("outer")
    z = inner // 2
    core = lax.rem(inner, 2)
    other = 1 - core
    up = {"inner": lax.rem(z + 1, ZS) * 2 + core}
    down = {"inner": lax.rem(z + ZS - 1, ZS) * 2 + core}
    mate = {"inner": z * 2 + other}

    def load_wide(src, dst, sem):
        for c in range(NCB):
            pltpu.make_async_copy(src.at[:, c * blk:(c + 1) * blk], dst.at[c], sem).start()

    pltpu.make_async_copy(act_hbm, act_v, load_sem.at[0]).start()
    load_wide(cot_hbm, cot_v, load_sem.at[1])
    w_copy = pltpu.make_async_copy(
        w_hbm.at[:, inner * OWN + outer // 2, pl.ds(lax.rem(outer, 2) * PIECE, PIECE), :], w_v, w_sem)
    w_copy.start()

    barrier = pltpu.get_barrier_semaphore()
    for peer in (up, down, mate):
        pl.semaphore_signal(barrier, inc=1, device_id=peer, device_id_type=MESH)
    for k in range(1, NOUT):
        pl.semaphore_signal(barrier, inc=1, device_id={"outer": lax.rem(outer + k, NOUT)}, device_id_type=MESH)
    pl.semaphore_wait(barrier, 3 + NOUT - 1)

    pltpu.make_async_copy(act_hbm, act_v, load_sem.at[0]).wait()
    pltpu.make_async_copy(act_hbm, cot_v, load_sem.at[1]).wait()
    pltpu.make_async_copy(gh_hbm, gh_v, load_sem.at[2]).start()
    load_wide(x_hbm, x_v, load_sem.at[3])

    def mate_copy(g):
        return pltpu.make_async_remote_copy(src_ref=psend.at[g], dst_ref=precv.at[g], send_sem=psend_sem.at[g],
                                            recv_sem=precv_sem.at[g], device_id=mate, device_id_type=MESH)

    def z_copy(q, slot):
        dst, sem = ((mid, mid_sem), (mid, mid_sem), (fin, fin_sem), (fin, fin_sem), (fin, fin_sem), (fin, fin_sem))[slot]
        k = (0, 1, 3, 1, 0, 2)[slot]
        peer = up if slot in (0, 2, 4) else down
        return pltpu.make_async_remote_copy(src_ref=zsend.at[q, slot], dst_ref=dst.at[q, k], send_sem=zsend_sem.at[q, slot],
                                            recv_sem=sem.at[q, k], device_id=peer, device_id_type=MESH)

    def grads(q, block0, dst):
        def four(i, _):
            for u in range(4):
                m = i * 4 + u
                n = block0 + m
                r = rows_ref[1 - q, n]
                c = cols_ref[1 - q, n]
                left = act_v[r] if q == 0 else x_v[r]
                right = cot_v[c] if q == 0 else gh_v[c]
                dst[m] = lax.dot_general(left, right, (((0,), (0,)), ((), ())),
                                         preferred_element_type=jnp.float32).astype(jnp.bfloat16)
            return 0
        lax.fori_loop(0, OWN // 4, four, 0)

    HALF = OWN // 2
    def chip(g, lo):
        part = slice(lo, lo + HALF)
        return own[g, part].astype(jnp.float32) + precv[g, part].astype(jnp.float32)

    def send_z(q, slot, value):
        zsend[q, slot] = value.astype(jnp.bfloat16)
        z_copy(q, slot).start()

    def process(q, d):
        g = q * ZS + d
        mate_copy(g).wait_recv()
        if d == 0:
            send_z(q, 0, chip(g, 0))
            send_z(q, 1, chip(g, HALF))
        elif d == 1:
            send_z(q, 2, chip(g, HALF))
        elif d == 2:
            send_z(q, 3, chip(g, 0))
        else:
            z_copy(q, 0).wait_recv()
            send_z(q, 4, chip(q * ZS + 1, 0) + mid[q, 0].astype(jnp.float32))
            z_copy(q, 1).wait_recv()
            send_z(q, 5, chip(q * ZS + 2, HALF) + mid[q, 1].astype(jnp.float32))

    def v_copy(q, k):
        to = lax.rem(outer + k, NOUT)
        return pltpu.make_async_remote_copy(src_ref=vsend.at[q, to], dst_ref=pieces.at[q, k], send_sem=vsend_sem.at[q, k],
                                            recv_sem=vrecv_sem.at[q, k], device_id={"outer": to}, device_id_type=MESH)

    def finish(q):
        for slot in (2, 3, 4, 5):
            z_copy(q, slot).wait_recv()
        g = q * ZS + 3
        for part in range(2):
            total = chip(g, part * HALF) + fin[q, 2 * part].astype(jnp.float32) + fin[q, 2 * part + 1].astype(jnp.float32)
            vsend[q, part * (NOUT // 2):(part + 1) * (NOUT // 2)] = total.astype(jnp.bfloat16).reshape(NOUT // 2, PIECE, blk)
        for k in range(1, NOUT):
            v_copy(q, k).start()
        keep = pltpu.make_async_copy(vsend.at[q, outer], pieces.at[q, 0], keep_sem.at[q])
        keep.start()

    for q in range(2):
        if q == 1:
            pltpu.make_async_copy(gh_hbm, gh_v, load_sem.at[2]).wait()
            pltpu.make_async_copy(gh_hbm, x_v, load_sem.at[3]).wait()
        for d in range(ZS):
            g = q * ZS + d
            owner = lax.rem(z + (2, 1, 3, 0)[d], ZS) * 2
            grads(q, (owner + other) * OWN, psend.at[g])
            mate_copy(g).start()
            grads(q, (owner + core) * OWN, own.at[g])
            if g > 0:
                process((g - 1) // ZS, (g - 1) % ZS)
    process(1, 3)
    finish(0)
    finish(1)

    def gram(q):
        for k in range(1, NOUT):
            v_copy(q, k).wait_recv()
        pltpu.make_async_copy(vsend.at[q, outer], pieces.at[q, 0], keep_sem.at[q]).wait()
        for s in range(NOUT):
            wide[q, s * PIECE:(s + 1) * PIECE] = pieces[q, lax.rem(outer - s + NOUT, NOUT)].astype(jnp.float32)
        picked = [wide[q, pl.ds(r, NOUT, stride=PIECE), :].astype(jnp.bfloat16) for r in range(PIECE)]
        flat = jnp.concatenate(picked, axis=1)
        return lax.dot_general(flat, flat, (((1,), (1,)), ((), ())), preferred_element_type=jnp.float32)

    g0 = gram(0)
    g1 = gram(1)
    gsend[...] = jnp.concatenate([g0, g1, jnp.zeros((NOUT, blk - 2 * NOUT), jnp.float32)], axis=1)

    def g_copy(k):
        to = lax.rem(outer + k, NOUT)
        return pltpu.make_async_remote_copy(src_ref=gsend, dst_ref=grecv.at[k - 1], send_sem=gsend_sem.at[k - 1],
                                            recv_sem=grecv_sem.at[k - 1], device_id={"outer": to}, device_id_type=MESH)
    for k in range(1, NOUT):
        g_copy(k).start()
    w_copy.wait()
    total = gsend[...]
    for k in range(1, NOUT):
        g_copy(k).wait_recv()
        total = total + grecv[k - 1]

    row = lax.broadcasted_iota(jnp.int32, (NOUT, NOUT), 0)
    lane = lax.broadcasted_iota(jnp.int32, (NOUT, NOUT), 1)
    for q in range(2):
        q_mat = total[:, q * NOUT:(q + 1) * NOUT]
        coef = jnp.ones((NOUT, 1), jnp.float32)
        step = 1
        while step < NOUT:
            same = row == lane
            pair = (row ^ step) == lane
            def mult(axis):
                norm = jnp.maximum(jnp.sum(jnp.where(same, q_mat, 0.0), axis=axis, keepdims=True), 0.0)
                cross = jnp.sum(jnp.where(pair, q_mat, 0.0), axis=axis, keepdims=True)
                return 1.0 - cross / (2.0 * (norm + dot_epsilon))
            mc, mr = mult(1), mult(0)
            coef = coef * mc
            q_mat = q_mat * mc * mr
            def partner(m, axis):
                parts = []
                for i in range(NOUT):
                    j = i ^ step
                    parts.append(m[j:j + 1, :] if axis == 0 else m[:, j:j + 1])
                return jnp.concatenate(parts, axis=axis)
            q_mat = q_mat + partner(q_mat, 0)
            q_mat = q_mat + partner(q_mat, 1)
            step *= 2
        comb = jnp.zeros((PIECE, blk), jnp.float32)
        for s in range(NOUT):
            comb = comb + coef[s:s + 1, :] * wide[q, s * PIECE:(s + 1) * PIECE]
        p = 1 - q
        new_m = momentum_decay * mom_ref[p] + comb
        outm_ref[p] = new_m
        outw_ref[p] = (w_v[p].astype(jnp.float32) - step_rate * new_m).astype(jnp.bfloat16)

    for g in range(2 * ZS):
        mate_copy(g).wait_send()
    for q in range(2):
        for slot in range(6):
            z_copy(q, slot).wait_send()
        for k in range(1, NOUT):
            v_copy(q, k).wait_send()
    for k in range(1, NOUT):
        g_copy(k).wait_send()


def combine(inputs, cotangent, activated, grad_hidden, weights, block_rows, block_cols, momentum):
    T = inputs.shape[0]
    blk = weights.shape[2]
    bf, f32 = jnp.bfloat16, jnp.float32
    smem = pl.BlockSpec(memory_space=pltpu.SMEM)
    hbm = pl.BlockSpec(memory_space=pl.ANY)
    vmem = pl.BlockSpec(memory_space=pltpu.VMEM)
    dma = pltpu.SemaphoreType.DMA
    V = pltpu.VMEM
    return pl.pallas_call(
        combine_kernel,
        in_specs=[smem, smem, hbm, hbm, hbm, hbm, hbm, vmem],
        out_specs=[vmem, vmem],
        out_shape=[jax.ShapeDtypeStruct(momentum.shape, bf), jax.ShapeDtypeStruct(momentum.shape, f32)],
        scratch_shapes=[
            V((NCB, T, blk), bf), V((NCB, T, blk), bf), V((NCB, T, blk), bf), V((NCB, T, blk), bf), V((2, PIECE, blk), bf),
            V((2 * ZS, OWN, blk, blk), bf), V((2 * ZS, OWN, blk, blk), bf), V((2 * ZS, OWN, blk, blk), bf),
            V((2, 6, OWN // 2, blk, blk), bf), V((2, 2, OWN // 2, blk, blk), bf), V((2, 4, OWN // 2, blk, blk), bf),
            V((2, NOUT, PIECE, blk), bf), V((2, NOUT, PIECE, blk), bf), V((2, NOUT * PIECE, blk), f32),
            V((NOUT, blk), f32), V((NOUT - 1, NOUT, blk), f32),
            dma((4,)), dma, dma((2,)), dma((2 * ZS,)), dma((2 * ZS,)), dma((2, 6)), dma((2, 2)), dma((2, 4)),
            dma((2, NOUT)), dma((2, NOUT)), dma((NOUT - 1,)), dma((NOUT - 1,)),
        ],
        compiler_params=pltpu.CompilerParams(vmem_limit_bytes=62 * 2**20, collective_id=0, has_side_effects=True),
        name="combine",
    )(block_rows, block_cols, inputs, cotangent, activated, grad_hidden, weights, momentum)


def local(inputs, cotangent, weights, block_rows, block_cols, momentum):
    activated, grad_hidden = forward(inputs, cotangent, weights, block_rows, block_cols)
    return tuple(combine(inputs, cotangent, activated, grad_hidden, weights, block_rows, block_cols, momentum))


def solution(mesh):
    return jax.shard_map(
        local,
        mesh=mesh,
        in_specs=(
            P(("inner", "outer"), None),
            P(("inner", "outer"), None),
            P(),
            P(),
            P(),
            P(None, ("inner", "outer"), None),
        ),
        out_specs=(P(None, ("inner", "outer"), None), P(None, ("inner", "outer"), None)),
        check_vma=False,
    )
```

time: 436 us -> 95 us (0.22)
  the two profiles are of different devices: /device:TPU:96 before, /device:TPU:0 now
where the time goes in v1:
time: 95 us; the launch traced here: 94.7 us
  Pallas kernels  91.2 us (96%)
  local copies, waits for them, and re-layouts  2.85 us (3%)
    pallas_call x1, Pallas kernels, combine(): pl.pallas_call(combine_kernel, in_specs=[smem, smem, hbm, hbm, hbm, hbm,...  48.8 us
    pallas_call x1, Pallas kernels, forward(): pl.pallas_call(functools.partial(forward_kernel, sub), grid=(T // tile,),...  42.3 us
    unnamed x2, local copies, waits for them, and re-layouts  2.85 us

profile of v1, /device:TPU:0, one launch (start us, length us, event | category | flops | bytes accessed | tf_op | source)
XLA Modules:
  0.0 94.7 jit_solution(15154566825215511489)
XLA Ops:
  0.6 42.3 %forward.1 = (bf16[32,1024,128]{2,1,0:T(8,128)(2,1)}, bf16[32,1024,128]{2,1,0:T(8,128)(2,1)}) custom-call(s32[2,64]{1,0:T(2,128)} %rows_ref.3, s32[2,64]{1,0:T(2,128)} %cols_ref.3, bf16[1024,4096]{1,0:T(8,128)(2,1)} %x_hbm.1, bf16[1024,4096]{1,0:T(8,128)(2,1)} %cot_hbm.1, bf16[2,64,128,128]{3,2,1,0:T(8,128)(2,1)} %w_hbm.1), custom_call_target="tpu_custom_call" | custom-call | tf_op jit(solution)/shard_map/forward/pallas_call | solution.py:85
  43.0 48.8 %combine.1 = (bf16[2,64,128]{2,1,0:T(8,128)(2,1)}, f32[2,64,128]{2,1,0:T(8,128)}) custom-call(s32[2,64]{1,0:T(2,128)} %rows_ref.3, s32[2,64]{1,0:T(2,128)} %cols_ref.3, bf16[1024,4096]{1,0:T(8,128)(2,1)} %x_hbm.1, bf16[1024,4096]{1,0:T(8,128)(2,1)} %cot_hbm.1, bf16[32,1024,128]{2,1,0:T(8,128)(2,1)} %get-tuple-element.4.act_hbm, ...), custom_call_target="tpu_custom_call" | custom-call | tf_op jit(solution)/shard_map/combine/pallas_call | solution.py:294
  91.8 1.4 %copy.10 = bf16[2,64,128]{2,1,0:T(8,128)(2,1)} copy(bf16[2,64,128]{2,1,0:T(8,128)(2,1)} %get-tuple-element.8) | data formatting | bytes 65536
  93.2 1.5 %copy.11 = f32[2,64,128]{2,1,0:T(8,128)} copy(f32[2,64,128]{2,1,0:T(8,128)} %get-tuple-element.9) | data formatting | bytes 131072

commit v2 on v1

v2 whole, which is shorter than its diff:
```python
import functools
import jax
import jax.numpy as jnp
from jax import lax
from jax.sharding import PartitionSpec as P
from jax.experimental import pallas as pl
from jax.experimental.pallas import tpu as pltpu
f32 = jnp.float32
bf = jnp.bfloat16
i32 = jnp.int32
dot_epsilon = 1e-06
momentum_decay = 0.9
step_rate = 0.05
NCB = 32
OWN = 8
ZS = 4
NOUT = 16
PIECE = 64
root_half = 0.7071067811865476
inv_root_tau = 0.3989422804014327

def forward_kernel(sub, rows_ref, cols_ref, x_hbm, cot_hbm, w_hbm, x_ref, cot_ref, act_ref, gh_ref,
                   head, link, seen, w_ref, extra_h, extra_a, sem, w_sem):
    blk = w_ref.shape[2]
    nb = w_ref.shape[1]
    tokens = x_ref.shape[1]

    w_loads = [pltpu.make_async_copy(w_hbm.at[p], w_ref.at[p], w_sem.at[p]) for p in range(2)]
    for load in w_loads:
        load.start()

    def clear(c, _):
        for p in range(2):
            head[p, c] = nb
            seen[p, c] = 0
        return 0
    lax.fori_loop(0, NCB, clear, 0)
    link[0, nb] = nb
    link[1, nb] = nb

    def push(n, _):
        c = cols_ref[0, n]
        link[0, n] = head[0, c]
        head[0, c] = n
        r = rows_ref[1, n]
        link[1, n] = head[1, r]
        head[1, r] = n
        return 0
    lax.fori_loop(0, nb, push, 0)

    def feature(p, n):
        return rows_ref[0, n] if p == 0 else cols_ref[1, n]

    def copy(p, f):
        src, dst = ((x_hbm, x_ref), (cot_hbm, cot_ref))[p]
        return pltpu.make_async_copy(src.at[:, pl.ds(pl.multiple_of(f * blk, blk), blk)], dst.at[f], sem.at[p, f])

    def fetch(c, _):
        for p in range(2):
            def one(n, p=p):
                f = feature(p, n)
                @pl.when(seen[p, f] == 0)
                def _():
                    seen[p, f] = 1
                    copy(p, f).start()
                return link[p, n]
            lax.while_loop(lambda n: n < nb, one, head[p, c])
        return 0
    lax.fori_loop(0, NCB, fetch, 0)
    for load in w_loads:
        load.wait()

    def arrive(p, f):
        @pl.when(seen[p, f] == 1)
        def _():
            seen[p, f] = 2
            copy(p, f).wait()

    def take(p, n):
        safe = jnp.minimum(n, nb - 1)
        w = w_ref[p, safe]
        return jnp.where(n < nb, w, jnp.zeros_like(w)), feature(p, safe)

    def pair(p, n, m):
        w1, f1 = take(p, n)
        w2, f2 = take(p, m)
        f2 = jnp.where(m < nb, f2, f1)
        return jnp.concatenate([w1, w2], axis=p), f1, f2

    def product(p, got, rows):
        w, f1, f2 = got
        ref = x_ref if p == 0 else cot_ref
        left = jnp.concatenate([ref[f1, rows, :], ref[f2, rows, :]], axis=1)
        return lax.dot_general(left, w, (((1,), (p,)), ((), ())), preferred_element_type=f32)

    def column(c, _):
        firsts, seconds, rests = [], [], []
        for p in range(2):
            def one(n, p=p):
                arrive(p, feature(p, n))
                return link[p, n]
            lax.while_loop(lambda n: n < nb, one, head[p, c])
            a = head[p, c]
            b = link[p, a]
            d = link[p, b]
            e = link[p, d]
            firsts.append((a, b))
            seconds.append((d, e))
            rests.append(link[p, e])
        @pl.when((firsts[0][0] == nb) | (firsts[1][0] == nb))
        def _():
            for p in range(2):
                arrive(p, feature(p, nb - 1))
        more = jnp.logical_or(rests[0] < nb, rests[1] < nb)
        two = [jnp.logical_or(seconds[p][0] < nb, more) for p in range(2)]

        def body(n0, n1, extra):
            gots = []
            for p, count in ((0, n0), (1, n1)):
                gots.append([pair(p, *firsts[p])] + ([pair(p, *seconds[p])] if count == 2 else []))
            for s in range(0, tokens, sub):
                rows = pl.ds(s, sub)
                h, g = (sum(product(p, got, rows) for got in gots[p]) for p in range(2))
                if extra:
                    h = h + extra_h[rows, :]
                    g = g + extra_a[rows, :]
                cum = 0.5 * (1.0 + lax.erf(h * root_half))
                act_ref[c, rows, :] = (h * cum).astype(bf)
                slope = cum + h * jnp.exp(-0.5 * h * h) * inv_root_tau
                gh_ref[c, rows, :] = (g * slope).astype(bf)

        for n0 in (1, 2):
            for n1 in (1, 2):
                @pl.when(jnp.logical_not(more) & (two[0] == (n0 == 2)) & (two[1] == (n1 == 2)))
                def _(n0=n0, n1=n1):
                    body(n0, n1, False)

        @pl.when(more)
        def _():
            for p, store in ((0, extra_h), (1, extra_a)):
                store[...] = jnp.zeros_like(store)
                def add(n, p=p, store=store):
                    m = link[p, n]
                    got = pair(p, n, m)
                    for s in range(0, tokens, sub):
                        store[pl.ds(s, sub), :] += product(p, got, pl.ds(s, sub))
                    return link[p, m]
                lax.while_loop(lambda n: n < nb, add, rests[p])
            body(2, 2, True)
        return 0
    lax.fori_loop(0, NCB, column, 0)


def forward(inputs, cotangent, weights, block_rows, block_cols, sub=256):
    T = inputs.shape[0]
    blk = weights.shape[2]
    nb = weights.shape[1]
    smem = pl.BlockSpec(memory_space=pltpu.SMEM)
    hbm = pl.BlockSpec(memory_space=pltpu.HBM)
    vmem = pl.BlockSpec(memory_space=pltpu.VMEM)
    return pl.pallas_call(
        functools.partial(forward_kernel, sub),
        in_specs=[smem, smem, hbm, hbm, hbm],
        out_specs=[vmem] * 4,
        out_shape=[pltpu.VMEM((NCB, T, blk), bf)] * 4,
        scratch_shapes=[
            pltpu.SMEM((2, NCB), jnp.int32), pltpu.SMEM((2, nb + 1), jnp.int32), pltpu.SMEM((2, NCB), jnp.int32),
            pltpu.VMEM(weights.shape, bf), pltpu.VMEM((T, blk), f32), pltpu.VMEM((T, blk), f32), pltpu.SemaphoreType.DMA((2, NCB)),
            pltpu.SemaphoreType.DMA((2,)),
        ],
        compiler_params=pltpu.CompilerParams(vmem_limit_bytes=26 * 2**20),
        name="forward",
    )(block_rows, block_cols, inputs, cotangent, weights)


def combine_kernel(rows_ref, cols_ref, x_v, cot_v, act_v, gh_v, out_ref,
                   psend, own, precv, zsend, mid, fin, vsend, pieces, wide, gsend, grecv,
                   keep_sem, psend_sem, precv_sem, zsend_sem, mid_sem, fin_sem, vsend_sem, vrecv_sem, gsend_sem, grecv_sem):
    MESH = pl.DeviceIdType.MESH
    blk = x_v.shape[2]
    inner = lax.axis_index("inner")
    outer = lax.axis_index("outer")
    z = inner // 2
    core = lax.rem(inner, 2)
    other = 1 - core
    up = {"inner": lax.rem(z + 1, ZS) * 2 + core}
    down = {"inner": lax.rem(z + ZS - 1, ZS) * 2 + core}
    mate = {"inner": z * 2 + other}

    barrier = pltpu.get_barrier_semaphore()
    for peer in (up, down, mate):
        pl.semaphore_signal(barrier, inc=1, device_id=peer, device_id_type=MESH)
    for k in range(1, NOUT):
        pl.semaphore_signal(barrier, inc=1, device_id={"outer": lax.rem(outer + k, NOUT)}, device_id_type=MESH)

    def mate_copy(g):
        return pltpu.make_async_remote_copy(src_ref=psend.at[g], dst_ref=precv.at[g], send_sem=psend_sem.at[g],
                                            recv_sem=precv_sem.at[g], device_id=mate, device_id_type=MESH)

    def z_copy(q, slot):
        dst, sem = ((mid, mid_sem), (mid, mid_sem), (fin, fin_sem), (fin, fin_sem), (fin, fin_sem), (fin, fin_sem))[slot]
        k = (0, 1, 3, 1, 0, 2)[slot]
        peer = up if slot in (0, 2, 4) else down
        return pltpu.make_async_remote_copy(src_ref=zsend.at[q, slot], dst_ref=dst.at[q, k], send_sem=zsend_sem.at[q, slot],
                                            recv_sem=sem.at[q, k], device_id=peer, device_id_type=MESH)

    def grads(q, block0, dst):
        def four(i, _):
            for u in range(4):
                m = i * 4 + u
                n = block0 + m
                r = rows_ref[1 - q, n]
                c = cols_ref[1 - q, n]
                left = act_v[r] if q == 0 else x_v[r]
                right = cot_v[c] if q == 0 else gh_v[c]
                dst[m] = lax.dot_general(left, right, (((0,), (0,)), ((), ())),
                                         preferred_element_type=f32).astype(bf)
            return 0
        lax.fori_loop(0, OWN // 4, four, 0)

    HALF = OWN // 2
    def chip(g, lo):
        part = slice(lo, lo + HALF)
        return own[g, part].astype(f32) + precv[g, part].astype(f32)

    def send_z(q, slot, value):
        zsend[q, slot] = value.astype(bf)
        z_copy(q, slot).start()

    def process(q, d):
        g = q * ZS + d
        mate_copy(g).wait_recv()
        if d == 0:
            send_z(q, 0, chip(g, 0))
            send_z(q, 1, chip(g, HALF))
        elif d == 1:
            send_z(q, 2, chip(g, HALF))
        elif d == 2:
            send_z(q, 3, chip(g, 0))
        else:
            z_copy(q, 0).wait_recv()
            send_z(q, 4, chip(q * ZS + 1, 0) + mid[q, 0].astype(f32))
            z_copy(q, 1).wait_recv()
            send_z(q, 5, chip(q * ZS + 2, HALF) + mid[q, 1].astype(f32))

    def v_copy(q, k):
        to = lax.rem(outer + k, NOUT)
        return pltpu.make_async_remote_copy(src_ref=vsend.at[q, to], dst_ref=pieces.at[q, k], send_sem=vsend_sem.at[q, k],
                                            recv_sem=vrecv_sem.at[q, k], device_id={"outer": to}, device_id_type=MESH)

    def finish(q):
        for slot in (2, 3, 4, 5):
            z_copy(q, slot).wait_recv()
        g = q * ZS + 3
        for part in range(2):
            total = chip(g, part * HALF) + fin[q, 2 * part].astype(f32) + fin[q, 2 * part + 1].astype(f32)
            vsend[q, part * (NOUT // 2):(part + 1) * (NOUT // 2)] = total.astype(bf).reshape(NOUT // 2, PIECE, blk)
        for k in range(1, NOUT):
            v_copy(q, k).start()
        keep = pltpu.make_async_copy(vsend.at[q, outer], pieces.at[q, 0], keep_sem.at[q])
        keep.start()

    for q in range(2):
        for d in range(ZS):
            g = q * ZS + d
            owner = lax.rem(z + (2, 1, 3, 0)[d], ZS) * 2
            grads(q, (owner + other) * OWN, psend.at[g])
            if g == 0:
                pl.semaphore_wait(barrier, 3 + NOUT - 1)
            mate_copy(g).start()
            grads(q, (owner + core) * OWN, own.at[g])
            if g > 0:
                process((g - 1) // ZS, (g - 1) % ZS)
    process(1, 3)
    finish(0)
    finish(1)

    def gram(q):
        for k in range(1, NOUT):
            v_copy(q, k).wait_recv()
        pltpu.make_async_copy(vsend.at[q, outer], pieces.at[q, 0], keep_sem.at[q]).wait()
        for s in range(NOUT):
            wide[q, s * PIECE:(s + 1) * PIECE] = pieces[q, lax.rem(outer - s + NOUT, NOUT)].astype(f32)
        picked = [wide[q, pl.ds(r, NOUT, stride=PIECE), :].astype(bf) for r in range(PIECE)]
        flat = jnp.concatenate(picked, axis=1)
        return lax.dot_general(flat, flat, (((1,), (1,)), ((), ())), preferred_element_type=f32)

    g0 = gram(0)
    g1 = gram(1)
    gsend[...] = jnp.concatenate([g0, g1, jnp.zeros((NOUT, blk - 2 * NOUT), f32)], axis=1)

    def g_copy(k):
        to = lax.rem(outer + k, NOUT)
        return pltpu.make_async_remote_copy(src_ref=gsend, dst_ref=grecv.at[k - 1], send_sem=gsend_sem.at[k - 1],
                                            recv_sem=grecv_sem.at[k - 1], device_id={"outer": to}, device_id_type=MESH)
    for k in range(1, NOUT):
        g_copy(k).start()
    total = gsend[...]
    for k in range(1, NOUT):
        g_copy(k).wait_recv()
        total = total + grecv[k - 1]

    row = lax.broadcasted_iota(jnp.int32, (NOUT, NOUT), 0)
    lane = lax.broadcasted_iota(jnp.int32, (NOUT, NOUT), 1)
    for q in range(2):
        q_mat = total[:, q * NOUT:(q + 1) * NOUT]
        coef = jnp.ones((NOUT, 1), f32)
        step = 1
        while step < NOUT:
            same = row == lane
            pair = (row ^ step) == lane
            def mult(axis):
                norm = jnp.maximum(jnp.sum(jnp.where(same, q_mat, 0.0), axis=axis, keepdims=True), 0.0)
                cross = jnp.sum(jnp.where(pair, q_mat, 0.0), axis=axis, keepdims=True)
                return 1.0 - cross / (2.0 * (norm + dot_epsilon))
            mc, mr = mult(1), mult(0)
            coef = coef * mc
            q_mat = q_mat * mc * mr
            def partner(m, axis):
                parts = []
                for i in range(NOUT):
                    j = i ^ step
                    parts.append(m[j:j + 1, :] if axis == 0 else m[:, j:j + 1])
                return jnp.concatenate(parts, axis=axis)
            q_mat = q_mat + partner(q_mat, 0)
            q_mat = q_mat + partner(q_mat, 1)
            step *= 2
        comb = jnp.zeros((PIECE, blk), f32)
        for s in range(NOUT):
            comb = comb + coef[s:s + 1, :] * wide[q, s * PIECE:(s + 1) * PIECE]
        out_ref[1 - q] = comb

    for g in range(2 * ZS):
        mate_copy(g).wait_send()
    for q in range(2):
        for slot in range(6):
            z_copy(q, slot).wait_send()
        for k in range(1, NOUT):
            v_copy(q, k).wait_send()
    for k in range(1, NOUT):
        g_copy(k).wait_send()


def combine(tokens, cots, activated, grad_hidden, block_rows, block_cols):
    blk = tokens.shape[2]
    smem = pl.BlockSpec(memory_space=pltpu.SMEM)
    vmem = pl.BlockSpec(memory_space=pltpu.VMEM)
    dma = pltpu.SemaphoreType.DMA
    V = pltpu.VMEM
    return pl.pallas_call(
        combine_kernel,
        in_specs=[smem, smem, vmem, vmem, vmem, vmem],
        out_specs=vmem,
        out_shape=jax.ShapeDtypeStruct((2, PIECE, blk), f32),
        scratch_shapes=[
            V((2 * ZS, OWN, blk, blk), bf), V((2 * ZS, OWN, blk, blk), bf), V((2 * ZS, OWN, blk, blk), bf),
            V((2, 6, OWN // 2, blk, blk), bf), V((2, 2, OWN // 2, blk, blk), bf), V((2, 4, OWN // 2, blk, blk), bf),
            V((2, NOUT, PIECE, blk), bf), V((2, NOUT, PIECE, blk), bf), V((2, NOUT * PIECE, blk), f32),
            V((NOUT, blk), f32), V((NOUT - 1, NOUT, blk), f32),
            dma((2,)), dma((2 * ZS,)), dma((2 * ZS,)), dma((2, 6)), dma((2, 2)), dma((2, 4)),
            dma((2, NOUT)), dma((2, NOUT)), dma((NOUT - 1,)), dma((NOUT - 1,)),
        ],
        compiler_params=pltpu.CompilerParams(vmem_limit_bytes=16 * 2**20, collective_id=0, has_side_effects=True),
        name="combine",
    )(block_rows, block_cols, tokens, cots, activated, grad_hidden)


def local(inputs, cotangent, weights, block_rows, block_cols, momentum):
    parts = forward(inputs, cotangent, weights, block_rows, block_cols)
    combined = combine(*parts, block_rows, block_cols)
    new_momentum = momentum_decay * momentum + combined
    place = lax.axis_index("inner") * NOUT + lax.axis_index("outer")
    held = lax.dynamic_slice_in_dim(weights.reshape(2, -1, weights.shape[3]), place * PIECE, PIECE, 1)
    new_weights = (held.astype(f32) - step_rate * new_momentum).astype(bf)
    return new_weights, new_momentum


def solution(mesh):
    return jax.shard_map(
        local,
        mesh=mesh,
        in_specs=(
            P(("inner", "outer"), None),
            P(("inner", "outer"), None),
            P(),
            P(),
            P(),
            P(None, ("inner", "outer"), None),
        ),
        out_specs=(P(None, ("inner", "outer"), None), P(None, ("inner", "outer"), None)),
        check_vma=False,
    )
```

time: 95 us -> 97.3 us (1.024); the launches traced: 94.7 us -> 95.6 us
  Pallas kernels: 91.2 us -> 73.7 us
  local copies, waits for them, and re-layouts: 2.85 us -> 19.8 us
  other arithmetic: 0 us -> 1.42 us
    pallas_call x2, Pallas kernels: 91.2 us -> 73.7 us  [the longest x1 45.1 us: combine(): pl.pallas_call(combine_kernel, in_specs=[smem, smem, vmem, vmem, vmem, vm...]
    unnamed x2 -> x18, local copies, waits for them, and re-layouts: 2.85 us -> 19.8 us
    convert_element_type x0 -> x1, other arithmetic: none -> 1.42 us  [local(): new_weights = (held.astype(f32) - step_rate * new_momentum).astype(bf)]
where the time goes in v2:
time: 97.3 us; the launch traced here: 95.6 us
  Pallas kernels  73.7 us (76%)
  local copies, waits for them, and re-layouts  19.8 us (20%)
  other arithmetic  1.42 us (1%)
    pallas_call x1, Pallas kernels, combine(): pl.pallas_call(combine_kernel, in_specs=[smem, smem, vmem, vmem, vmem, vm...  45.1 us
    pallas_call x1, Pallas kernels, forward(): pl.pallas_call(functools.partial(forward_kernel, sub), in_specs=[smem, sm...  28.6 us
    unnamed x18, local copies, waits for them, and re-layouts  19.8 us

profile of v2, /device:TPU:0, one launch (start us, length us, event | category | flops | bytes accessed | tf_op | source)
XLA Modules:
  0.0 95.6 jit_solution(9309272776161479619)
XLA Ops:
  0.6 0.0 copy-start.7
  0.6 0.0 copy-start.6
  0.7 28.6 %forward.1 = (bf16[32,1024,128]{2,1,0:T(8,128)(2,1)S(1)}, bf16[32,1024,128]{2,1,0:T(8,128)(2,1)S(1)}, bf16[32,1024,128]{2,1,0:T(8,128)(2,1)S(1)}, bf16[32,1024,128]{2,1,0:T(8,128)(2,1)S(1)}) custom-call(s32[2,64]{1,0:T(2,128)} %rows_ref.3, s32[2,64]{1,0:T(2,128)} %cols_ref.3, bf16[1024,4096]{1,0:T(8,128)(2,1)} %x_hbm.1, bf16[1024,4096]{1,0:T(8,128)(2,1)} %cot_hbm.1, ...), custom_call_target="tpu_custom_call" | custom-call | tf_op jit(solution)/shard_map/forward/pallas_call | solution.py:161
  29.2 0.0 copy-start
  29.2 3.2 %copy-done = bf16[32,1024,128]{2,1,0:T(8,128)(2,1)} copy-done((bf16[32,1024,128]{2,1,0:T(8,128)(2,1)}, bf16[32,1024,128]{2,1,0:T(8,128)(2,1)S(1)}, u32[]{:S(2)}) %copy-start) | copy-done | bytes 8388632
  32.5 0.0 copy-start.2
  32.5 3.2 %copy-done.2 = bf16[32,1024,128]{2,1,0:T(8,128)(2,1)} copy-done((bf16[32,1024,128]{2,1,0:T(8,128)(2,1)}, bf16[32,1024,128]{2,1,0:T(8,128)(2,1)S(1)}, u32[]{:S(2)}) %copy-start.2) | copy-done | bytes 8388632
  35.7 0.0 copy-start.4
  35.7 3.2 %copy-done.4 = bf16[32,1024,128]{2,1,0:T(8,128)(2,1)} copy-done((bf16[32,1024,128]{2,1,0:T(8,128)(2,1)}, bf16[32,1024,128]{2,1,0:T(8,128)(2,1)S(1)}, u32[]{:S(2)}) %copy-start.4) | copy-done | bytes 8388632
  38.9 0.0 copy-done.7
  38.9 0.0 copy-done.6
  38.9 0.0 copy-start.1
  38.9 3.4 %copy-done.1 = bf16[32,1024,128]{2,1,0:T(8,128)(2,1)S(1)} copy-done((bf16[32,1024,128]{2,1,0:T(8,128)(2,1)S(1)}, bf16[32,1024,128]{2,1,0:T(8,128)(2,1)}, u32[]{:S(2)}) %copy-start.1) | copy-done | bytes 8388632
  42.3 0.0 copy-start.3
  42.3 3.4 %copy-done.3 = bf16[32,1024,128]{2,1,0:T(8,128)(2,1)S(1)} copy-done((bf16[32,1024,128]{2,1,0:T(8,128)(2,1)S(1)}, bf16[32,1024,128]{2,1,0:T(8,128)(2,1)}, u32[]{:S(2)}) %copy-start.3) | copy-done | bytes 8388632
  45.7 0.0 copy-start.5
  45.7 3.4 %copy-done.5 = bf16[32,1024,128]{2,1,0:T(8,128)(2,1)S(1)} copy-done((bf16[32,1024,128]{2,1,0:T(8,128)(2,1)S(1)}, bf16[32,1024,128]{2,1,0:T(8,128)(2,1)}, u32[]{:S(2)}) %copy-start.5) | copy-done | bytes 8388632
  49.1 0.0 copy-start.8
  49.1 45.1 %combine.1 = f32[2,64,128]{2,1,0:T(8,128)S(1)} custom-call(s32[2,64]{1,0:T(2,128)S(1)} %copy-done.6, s32[2,64]{1,0:T(2,128)S(1)} %copy-done.7, bf16[32,1024,128]{2,1,0:T(8,128)(2,1)S(1)} %copy-done.1, bf16[32,1024,128]{2,1,0:T(8,128)(2,1)S(1)} %copy-done.3, bf16[32,1024,128]{2,1,0:T(8,128)(2,1)S(1)} %copy-done.5, ...), custom_call_target="tpu_custom_call" | custom-call | tf_op jit(solution)/shard_map/combine/pallas_call | solution.py:350
  94.2 0.0 copy-done.8
  94.2 1.4 %subtract_convert_fusion = (bf16[2,64,128]{2,1,0:T(8,128)(2,1)}, f32[2,64,128]{2,1,0:T(8,128)}) fusion(bf16[2,8192,128]{2,1,0:T(8,128)(2,1)} %bitcast.1, s32[]{:T(128)S(6)} %select_n.3, f32[2,64,128]{2,1,0:T(8,128)S(1)} %combine.1, f32[2,64,128]{2,1,0:T(8,128)S(1)} %copy-done.8), kind=kLoop, calls=%fused_computation | loop fusion | flops 98304 | bytes 262148 | tf_op jit(solution)/shard_map/convert_element_type | solution.py:374
Async XLA Ops:
  0.6 38.3 %copy-start.7 = (s32[2,64]{1,0:T(2,128)S(1)}, s32[2,64]{1,0:T(2,128)}, u32[]{:S(2)}) copy-start(s32[2,64]{1,0:T(2,128)} %cols_ref.3) | copy-start | bytes 1540
  0.6 38.3 %copy-start.6 = (s32[2,64]{1,0:T(2,128)S(1)}, s32[2,64]{1,0:T(2,128)}, u32[]{:S(2)}) copy-start(s32[2,64]{1,0:T(2,128)} %rows_ref.3) | copy-start | bytes 1540
  29.2 3.2 %copy-start = (bf16[32,1024,128]{2,1,0:T(8,128)(2,1)}, bf16[32,1024,128]{2,1,0:T(8,128)(2,1)S(1)}, u32[]{:S(2)}) copy-start(bf16[32,1024,128]{2,1,0:T(8,128)(2,1)S(1)} %get-tuple-element.6.x_v) | copy-start | bytes 25165828
  32.5 3.2 %copy-start.2 = (bf16[32,1024,128]{2,1,0:T(8,128)(2,1)}, bf16[32,1024,128]{2,1,0:T(8,128)(2,1)S(1)}, u32[]{:S(2)}) copy-start(bf16[32,1024,128]{2,1,0:T(8,128)(2,1)S(1)} %get-tuple-element.7.cot_v) | copy-start | bytes 25165828
  35.7 3.2 %copy-start.4 = (bf16[32,1024,128]{2,1,0:T(8,128)(2,1)}, bf16[32,1024,128]{2,1,0:T(8,128)(2,1)S(1)}, u32[]{:S(2)}) copy-start(bf16[32,1024,128]{2,1,0:T(8,128)(2,1)S(1)} %get-tuple-element.8.act_v) | copy-start | bytes 25165828
  38.9 3.4 %copy-start.1 = (bf16[32,1024,128]{2,1,0:T(8,128)(2,1)S(1)}, bf16[32,1024,128]{2,1,0:T(8,128)(2,1)}, u32[]{:S(2)}) copy-start(bf16[32,1024,128]{2,1,0:T(8,128)(2,1)} %copy-done) | copy-start | bytes 25165828
  42.3 3.4 %copy-start.3 = (bf16[32,1024,128]{2,1,0:T(8,128)(2,1)S(1)}, bf16[32,1024,128]{2,1,0:T(8,128)(2,1)}, u32[]{:S(2)}) copy-start(bf16[32,1024,128]{2,1,0:T(8,128)(2,1)} %copy-done.2) | copy-start | bytes 25165828
  45.7 3.4 %copy-start.5 = (bf16[32,1024,128]{2,1,0:T(8,128)(2,1)S(1)}, bf16[32,1024,128]{2,1,0:T(8,128)(2,1)}, u32[]{:S(2)}) copy-start(bf16[32,1024,128]{2,1,0:T(8,128)(2,1)} %copy-done.4) | copy-start | bytes 25165828
  49.1 45.1 %copy-start.8 = (f32[2,64,128]{2,1,0:T(8,128)S(1)}, f32[2,64,128]{2,1,0:T(8,128)}, u32[]{:S(2)}) copy-start(f32[2,64,128]{2,1,0:T(8,128)} %param.11) | copy-start | bytes 196612

commit v3 on v2

--- a/solution.py
+++ b/solution.py
@@ -34,7 +34,7 @@
             head[p, c] = nb
             seen[p, c] = 0
         return 0
-    lax.fori_loop(0, NCB, clear, 0)
+    lax.fori_loop(0, NCB, clear, 0, unroll=True)
     link[0, nb] = nb
     link[1, nb] = nb
 
@@ -46,7 +46,7 @@
         link[1, n] = head[1, r]
         head[1, r] = n
         return 0
-    lax.fori_loop(0, nb, push, 0)
+    lax.fori_loop(0, nb, push, 0, unroll=8)
 
     def feature(p, n):
         return rows_ref[0, n] if p == 0 else cols_ref[1, n]
@@ -205,18 +205,13 @@
                                             recv_sem=sem.at[q, k], device_id=peer, device_id_type=MESH)
 
     def grads(q, block0, dst):
-        def four(i, _):
-            for u in range(4):
-                m = i * 4 + u
-                n = block0 + m
-                r = rows_ref[1 - q, n]
-                c = cols_ref[1 - q, n]
-                left = act_v[r] if q == 0 else x_v[r]
-                right = cot_v[c] if q == 0 else gh_v[c]
-                dst[m] = lax.dot_general(left, right, (((0,), (0,)), ((), ())),
-                                         preferred_element_type=f32).astype(bf)
-            return 0
-        lax.fori_loop(0, OWN // 4, four, 0)
+        for m in range(OWN):
+            n = block0 + m
+            r = rows_ref[1 - q, n]
+            c = cols_ref[1 - q, n]
+            left = act_v[r] if q == 0 else x_v[r]
+            right = cot_v[c] if q == 0 else gh_v[c]
+            dst[m] = lax.dot_general(left, right, (((0,), (0,)), ((), ())), preferred_element_type=f32).astype(bf)
 
     HALF = OWN // 2
     def chip(g, lo):

time: 97.3 us -> 95.9 us (0.986); the launches traced: 95.6 us -> 96.8 us
  Pallas kernels: 73.7 us -> 74.9 us
    pallas_call x1, Pallas kernels: 28.6 us -> 31.1 us  [forward(): pl.pallas_call(functools.partial(forward_kernel, sub), in_specs=[smem, sm...]
    pallas_call x1, Pallas kernels: 45.1 us -> 43.8 us  [combine(): pl.pallas_call(combine_kernel, in_specs=[smem, smem, vmem, vmem, vmem, vm...]
where the time goes in v3:
time: 95.9 us; the launch traced here: 96.8 us
  Pallas kernels  74.9 us (78%)
  local copies, waits for them, and re-layouts  19.8 us (21%)
  other arithmetic  1.42 us (1%)
    pallas_call x1, Pallas kernels, combine(): pl.pallas_call(combine_kernel, in_specs=[smem, smem, vmem, vmem, vmem, vm...  43.8 us
    pallas_call x1, Pallas kernels, forward(): pl.pallas_call(functools.partial(forward_kernel, sub), in_specs=[smem, sm...  31.1 us
    unnamed x18, local copies, waits for them, and re-layouts  19.8 us

profile of v3, /device:TPU:0, one launch (start us, length us, event | category | flops | bytes accessed | tf_op | source)
XLA Modules:
  0.0 96.8 jit_solution(8434072118310915848)
XLA Ops:
  0.6 0.0 copy-start.7
  0.6 0.0 copy-start.6
  0.7 31.1 %forward.1 = (bf16[32,1024,128]{2,1,0:T(8,128)(2,1)S(1)}, bf16[32,1024,128]{2,1,0:T(8,128)(2,1)S(1)}, bf16[32,1024,128]{2,1,0:T(8,128)(2,1)S(1)}, bf16[32,1024,128]{2,1,0:T(8,128)(2,1)S(1)}) custom-call(s32[2,64]{1,0:T(2,128)} %rows_ref.3, s32[2,64]{1,0:T(2,128)} %cols_ref.3, bf16[1024,4096]{1,0:T(8,128)(2,1)} %x_hbm.1, bf16[1024,4096]{1,0:T(8,128)(2,1)} %cot_hbm.1, ...), custom_call_target="tpu_custom_call" | custom-call | tf_op jit(solution)/shard_map/forward/pallas_call | solution.py:161
  31.7 0.0 copy-start
  31.7 3.2 %copy-done = bf16[32,1024,128]{2,1,0:T(8,128)(2,1)} copy-done((bf16[32,1024,128]{2,1,0:T(8,128)(2,1)}, bf16[32,1024,128]{2,1,0:T(8,128)(2,1)S(1)}, u32[]{:S(2)}) %copy-start) | copy-done | bytes 8388632
  35.0 0.0 copy-start.2
  35.0 3.2 %copy-done.2 = bf16[32,1024,128]{2,1,0:T(8,128)(2,1)} copy-done((bf16[32,1024,128]{2,1,0:T(8,128)(2,1)}, bf16[32,1024,128]{2,1,0:T(8,128)(2,1)S(1)}, u32[]{:S(2)}) %copy-start.2) | copy-done | bytes 8388632
  38.2 0.0 copy-start.4
  38.2 3.2 %copy-done.4 = bf16[32,1024,128]{2,1,0:T(8,128)(2,1)} copy-done((bf16[32,1024,128]{2,1,0:T(8,128)(2,1)}, bf16[32,1024,128]{2,1,0:T(8,128)(2,1)S(1)}, u32[]{:S(2)}) %copy-start.4) | copy-done | bytes 8388632
  41.4 0.0 copy-done.7
  41.4 0.0 copy-done.6
  41.4 0.0 copy-start.1
  41.4 3.4 %copy-done.1 = bf16[32,1024,128]{2,1,0:T(8,128)(2,1)S(1)} copy-done((bf16[32,1024,128]{2,1,0:T(8,128)(2,1)S(1)}, bf16[32,1024,128]{2,1,0:T(8,128)(2,1)}, u32[]{:S(2)}) %copy-start.1) | copy-done | bytes 8388632
  44.8 0.0 copy-start.3
  44.8 3.4 %copy-done.3 = bf16[32,1024,128]{2,1,0:T(8,128)(2,1)S(1)} copy-done((bf16[32,1024,128]{2,1,0:T(8,128)(2,1)S(1)}, bf16[32,1024,128]{2,1,0:T(8,128)(2,1)}, u32[]{:S(2)}) %copy-start.3) | copy-done | bytes 8388632
  48.2 0.0 copy-start.5
  48.2 3.4 %copy-done.5 = bf16[32,1024,128]{2,1,0:T(8,128)(2,1)S(1)} copy-done((bf16[32,1024,128]{2,1,0:T(8,128)(2,1)S(1)}, bf16[32,1024,128]{2,1,0:T(8,128)(2,1)}, u32[]{:S(2)}) %copy-start.5) | copy-done | bytes 8388632
  51.6 0.0 copy-start.8
  51.6 43.8 %combine.1 = f32[2,64,128]{2,1,0:T(8,128)S(1)} custom-call(s32[2,64]{1,0:T(2,128)S(1)} %copy-done.6, s32[2,64]{1,0:T(2,128)S(1)} %copy-done.7, bf16[32,1024,128]{2,1,0:T(8,128)(2,1)S(1)} %copy-done.1, bf16[32,1024,128]{2,1,0:T(8,128)(2,1)S(1)} %copy-done.3, bf16[32,1024,128]{2,1,0:T(8,128)(2,1)S(1)} %copy-done.5, ...), custom_call_target="tpu_custom_call" | custom-call | tf_op jit(solution)/shard_map/combine/pallas_call | solution.py:345
  95.4 0.0 copy-done.8
  95.4 1.4 %subtract_convert_fusion = (bf16[2,64,128]{2,1,0:T(8,128)(2,1)}, f32[2,64,128]{2,1,0:T(8,128)}) fusion(bf16[2,8192,128]{2,1,0:T(8,128)(2,1)} %bitcast.1, s32[]{:T(128)S(6)} %select_n.3, f32[2,64,128]{2,1,0:T(8,128)S(1)} %combine.1, f32[2,64,128]{2,1,0:T(8,128)S(1)} %copy-done.8), kind=kLoop, calls=%fused_computation | loop fusion | flops 98304 | bytes 262148 | tf_op jit(solution)/shard_map/convert_element_type | solution.py:369
Async XLA Ops:
  0.6 40.8 %copy-start.7 = (s32[2,64]{1,0:T(2,128)S(1)}, s32[2,64]{1,0:T(2,128)}, u32[]{:S(2)}) copy-start(s32[2,64]{1,0:T(2,128)} %cols_ref.3) | copy-start | bytes 1540
  0.6 40.8 %copy-start.6 = (s32[2,64]{1,0:T(2,128)S(1)}, s32[2,64]{1,0:T(2,128)}, u32[]{:S(2)}) copy-start(s32[2,64]{1,0:T(2,128)} %rows_ref.3) | copy-start | bytes 1540
  31.7 3.2 %copy-start = (bf16[32,1024,128]{2,1,0:T(8,128)(2,1)}, bf16[32,1024,128]{2,1,0:T(8,128)(2,1)S(1)}, u32[]{:S(2)}) copy-start(bf16[32,1024,128]{2,1,0:T(8,128)(2,1)S(1)} %get-tuple-element.6.x_v) | copy-start | bytes 25165828
  35.0 3.2 %copy-start.2 = (bf16[32,1024,128]{2,1,0:T(8,128)(2,1)}, bf16[32,1024,128]{2,1,0:T(8,128)(2,1)S(1)}, u32[]{:S(2)}) copy-start(bf16[32,1024,128]{2,1,0:T(8,128)(2,1)S(1)} %get-tuple-element.7.cot_v) | copy-start | bytes 25165828
  38.2 3.2 %copy-start.4 = (bf16[32,1024,128]{2,1,0:T(8,128)(2,1)}, bf16[32,1024,128]{2,1,0:T(8,128)(2,1)S(1)}, u32[]{:S(2)}) copy-start(bf16[32,1024,128]{2,1,0:T(8,128)(2,1)S(1)} %get-tuple-element.8.act_v) | copy-start | bytes 25165828
  41.4 3.4 %copy-start.1 = (bf16[32,1024,128]{2,1,0:T(8,128)(2,1)S(1)}, bf16[32,1024,128]{2,1,0:T(8,128)(2,1)}, u32[]{:S(2)}) copy-start(bf16[32,1024,128]{2,1,0:T(8,128)(2,1)} %copy-done) | copy-start | bytes 25165828
  44.8 3.4 %copy-start.3 = (bf16[32,1024,128]{2,1,0:T(8,128)(2,1)S(1)}, bf16[32,1024,128]{2,1,0:T(8,128)(2,1)}, u32[]{:S(2)}) copy-start(bf16[32,1024,128]{2,1,0:T(8,128)(2,1)} %copy-done.2) | copy-start | bytes 25165828
  48.2 3.4 %copy-start.5 = (bf16[32,1024,128]{2,1,0:T(8,128)(2,1)S(1)}, bf16[32,1024,128]{2,1,0:T(8,128)(2,1)}, u32[]{:S(2)}) copy-start(bf16[32,1024,128]{2,1,0:T(8,128)(2,1)} %copy-done.4) | copy-start | bytes 25165828
  51.6 43.8 %copy-start.8 = (f32[2,64,128]{2,1,0:T(8,128)S(1)}, f32[2,64,128]{2,1,0:T(8,128)}, u32[]{:S(2)}) copy-start(f32[2,64,128]{2,1,0:T(8,128)} %param.11) | copy-start | bytes 196612

commit v4 on v3

--- a/solution.py
+++ b/solution.py
@@ -168,7 +168,7 @@
             pltpu.VMEM(weights.shape, bf), pltpu.VMEM((T, blk), f32), pltpu.VMEM((T, blk), f32), pltpu.SemaphoreType.DMA((2, NCB)),
             pltpu.SemaphoreType.DMA((2,)),
         ],
-        compiler_params=pltpu.CompilerParams(vmem_limit_bytes=26 * 2**20),
+        compiler_params=pltpu.CompilerParams(vmem_limit_bytes=20 * 2**20),
         name="forward",
     )(block_rows, block_cols, inputs, cotangent, weights)
 
@@ -263,9 +263,9 @@
             if g == 0:
                 pl.semaphore_wait(barrier, 3 + NOUT - 1)
             mate_copy(g).start()
-            grads(q, (owner + core) * OWN, own.at[g])
             if g > 0:
                 process((g - 1) // ZS, (g - 1) % ZS)
+            grads(q, (owner + core) * OWN, own.at[g])
     process(1, 3)
     finish(0)
     finish(1)
@@ -295,34 +295,35 @@
         g_copy(k).wait_recv()
         total = total + grecv[k - 1]
 
-    row = lax.broadcasted_iota(jnp.int32, (NOUT, NOUT), 0)
-    lane = lax.broadcasted_iota(jnp.int32, (NOUT, NOUT), 1)
+    q_mat = jnp.concatenate([total, pltpu.roll(total, blk - NOUT, 1)], axis=0)
+    row = lax.broadcasted_iota(jnp.int32, (2 * NOUT, blk), 0)
+    lane = lax.broadcasted_iota(jnp.int32, (2 * NOUT, blk), 1)
+    place = row % NOUT
+    coef = jnp.ones((2 * NOUT, 1), f32)
+    step = 1
+    while step < NOUT:
+        same = place == lane
+        pair = (place ^ step) == lane
+
+        def mult(norm, cross):
+            return 1.0 - cross / (2.0 * (jnp.maximum(norm, 0.0) + dot_epsilon))
+        norms = jnp.where(same, q_mat, 0.0)
+        crosses = jnp.where(pair, q_mat, 0.0)
+        mc = mult(jnp.sum(norms, axis=1, keepdims=True), jnp.sum(crosses, axis=1, keepdims=True))
+        mr = jnp.concatenate([
+            jnp.broadcast_to(mult(jnp.sum(norms[h:h + NOUT], axis=0, keepdims=True),
+                                  jnp.sum(crosses[h:h + NOUT], axis=0, keepdims=True)), (NOUT, blk))
+            for h in (0, NOUT)], axis=0)
+        coef = coef * mc
+        q_mat = q_mat * mc * mr
+        for axis, index in ((0, row), (1, lane)):
+            size = q_mat.shape[axis]
+            q_mat = q_mat + jnp.where((index & step) > 0, pltpu.roll(q_mat, step, axis), pltpu.roll(q_mat, size - step, axis))
+        step *= 2
     for q in range(2):
-        q_mat = total[:, q * NOUT:(q + 1) * NOUT]
-        coef = jnp.ones((NOUT, 1), f32)
-        step = 1
-        while step < NOUT:
-            same = row == lane
-            pair = (row ^ step) == lane
-            def mult(axis):
-                norm = jnp.maximum(jnp.sum(jnp.where(same, q_mat, 0.0), axis=axis, keepdims=True), 0.0)
-                cross = jnp.sum(jnp.where(pair, q_mat, 0.0), axis=axis, keepdims=True)
-                return 1.0 - cross / (2.0 * (norm + dot_epsilon))
-            mc, mr = mult(1), mult(0)
-            coef = coef * mc
-            q_mat = q_mat * mc * mr
-            def partner(m, axis):
-                parts = []
-                for i in range(NOUT):
-                    j = i ^ step
-                    parts.append(m[j:j + 1, :] if axis == 0 else m[:, j:j + 1])
-                return jnp.concatenate(parts, axis=axis)
-            q_mat = q_mat + partner(q_mat, 0)
-            q_mat = q_mat + partner(q_mat, 1)
-            step *= 2
         comb = jnp.zeros((PIECE, blk), f32)
         for s in range(NOUT):
-            comb = comb + coef[s:s + 1, :] * wide[q, s * PIECE:(s + 1) * PIECE]
+            comb = comb + coef[q * NOUT + s:q * NOUT + s + 1, :] * wide[q, s * PIECE:(s + 1) * PIECE]
         out_ref[1 - q] = comb
 
     for g in range(2 * ZS):

time: 95.9 us -> 74 us (0.77)
  local copies, waits for them, and re-layouts: 19.8 us -> 1.36 us
  Pallas kernels: 74.9 us -> 70.5 us
    unnamed x18 -> x6, local copies, waits for them, and re-layouts: 19.8 us -> 1.36 us
    pallas_call x1, Pallas kernels: 31.1 us -> 26.8 us  [forward(): pl.pallas_call(functools.partial(forward_kernel, sub), in_specs=[smem, sm...]
where the time goes in v4:
time: 74 us
  Pallas kernels  70.5 us (95%)
  other arithmetic  1.41 us (2%)
  local copies, waits for them, and re-layouts  1.36 us (2%)
    pallas_call x1, Pallas kernels, combine(): pl.pallas_call(combine_kernel, in_specs=[smem, smem, vmem, vmem, vmem, vm...  43.8 us
    pallas_call x1, Pallas kernels, forward(): pl.pallas_call(functools.partial(forward_kernel, sub), in_specs=[smem, sm...  26.8 us

profile of v4, /device:TPU:0, one launch (start us, length us, event | category | flops | bytes accessed | tf_op | source)
XLA Modules:
  0.0 74.0 jit_solution(13384523720355346071)
XLA Ops:
  0.6 0.0 copy-start
  0.6 0.7 copy-done
  1.3 0.0 copy-start.1
  1.3 0.7 copy-done.1
  2.0 26.8 %forward.1 = (bf16[32,1024,128]{2,1,0:T(8,128)(2,1)S(1)}, bf16[32,1024,128]{2,1,0:T(8,128)(2,1)S(1)}, bf16[32,1024,128]{2,1,0:T(8,128)(2,1)S(1)}, bf16[32,1024,128]{2,1,0:T(8,128)(2,1)S(1)}) custom-call(s32[2,64]{1,0:T(2,128)S(1)} %copy-done, s32[2,64]{1,0:T(2,128)S(1)} %copy-done.1, bf16[1024,4096]{1,0:T(8,128)(2,1)} %x_hbm.1, bf16[1024,4096]{1,0:T(8,128)(2,1)} %cot_hbm.1, ...), custom_call_target="tpu_custom_call" | custom-call | tf_op jit(solution)/shard_map/forward/pallas_call | solution.py:161
  28.8 0.0 copy-start.2
  28.8 43.8 %combine.1 = f32[2,64,128]{2,1,0:T(8,128)S(1)} custom-call(s32[2,64]{1,0:T(2,128)S(1)} %copy-done, s32[2,64]{1,0:T(2,128)S(1)} %copy-done.1, bf16[32,1024,128]{2,1,0:T(8,128)(2,1)S(1)} %get-tuple-element.6.x_v, bf16[32,1024,128]{2,1,0:T(8,128)(2,1)S(1)} %get-tuple-element.7.cot_v, bf16[32,1024,128]{2,1,0:T(8,128)(2,1)S(1)} %get-tuple-element.8.act_v, ...), custom_call_target="tpu_custom_call" | custom-call | tf_op jit(solution)/shard_map/combine/pallas_call | solution.py:346
  72.5 0.0 copy-done.2
  72.5 1.4 %subtract_convert_fusion = (bf16[2,64,128]{2,1,0:T(8,128)(2,1)}, f32[2,64,128]{2,1,0:T(8,128)}) fusion(bf16[2,8192,128]{2,1,0:T(8,128)(2,1)} %bitcast.1, s32[]{:T(128)S(6)} %select_n.3, f32[2,64,128]{2,1,0:T(8,128)S(1)} %combine.1, f32[2,64,128]{2,1,0:T(8,128)S(1)} %copy-done.2), kind=kLoop, calls=%fused_computation | loop fusion | flops 98304 | bytes 262148 | tf_op jit(solution)/shard_map/convert_element_type | solution.py:370
Async XLA Ops:
  0.6 0.7 copy-start
  1.3 0.7 copy-start.1
  28.8 43.8 %copy-start.2 = (f32[2,64,128]{2,1,0:T(8,128)S(1)}, f32[2,64,128]{2,1,0:T(8,128)}, u32[]{:S(2)}) copy-start(f32[2,64,128]{2,1,0:T(8,128)} %param.11) | copy-start | bytes 196612
